TPU v7x, 32 devices: a whole 2x2x4 slice. The times are simulated.
32 devices in a mesh: seq: 8 (over y, x, core), vid: 4 (over z).
Axes of the slice: x: 2, y: 2, z: 4, core: 2. Of those that a mesh axis runs over, the one named last changes fastest.
Arguments:
- tokens: bfloat16 [32768, 768], P(('vid', 'seq')), parts along dimension 0, may hold values from -100 to 100
- latents: bfloat16 [2048, 768], P(('vid', 'seq')), parts along dimension 0, may hold values from -6 to 6
- read_weights: bfloat16 [4, 768, 768], P(None, 'seq'), may hold values from -1 to 1
- later_weights: bfloat16 [8, 768, 768], P(None, 'seq'), may hold values from -1 to 1
- head_scale: float32 [3, 12], replicated, may hold values from 1 to 40
Outputs:
- tokens_out: bfloat16 [32768, 768], P(('vid', 'seq')), parts along dimension 0
- latents_out: float32 [2048, 768], P(('vid', 'seq')), parts along dimension 0
There are 4 independent parts, one for each index of `vid`. A program takes and returns all parts, laid end to end along the dimension named above; an argument that names none is the same for every part. Nothing has to cross between parts.
All inputs are finite; a program needn't handle non-finite values.
Results may differ from a plain program's by a relative error of at most 0.01.
The roundings to bfloat16 on the way count: a program that leaves them out, or rounds other values in their place, can miss the bound.
Values may be sent and summed in bfloat16 or wider, within the bound.
A program may use at most 64 MiB of HBM per device.

v0:
```python
import math

import jax
import jax.numpy as jnp
from jax import lax
from jax.sharding import PartitionSpec as P

HEADS = 12


epsilon = 1e-06


def norm_rows(values):
    values = values.astype(jnp.float32)
    return values * lax.rsqrt(jnp.mean(values * values, axis=-1, keepdims=True) + epsilon)


def head_norm(values, n_heads):
    by_head = values.reshape(values.shape[0], n_heads, values.shape[1] // n_heads)
    by_head = by_head * lax.rsqrt(jnp.mean(by_head * by_head, axis=-1, keepdims=True) + epsilon)
    return by_head.reshape(values.shape).astype(jnp.bfloat16)


def project(inputs, weight):
    return jnp.dot(inputs, weight, preferred_element_type=jnp.float32)


def head_cols(values, head_index, head_dim):
    return lax.dynamic_slice_in_dim(values, head_index * head_dim, head_dim, 1)


def inner(left, right):
    return lax.dot_general(
        left, right, (((1,), (1,)), ((), ())), preferred_element_type=jnp.float32
    )


def attend(queries, key_rows, val_rows, factors, n_heads):
    head_dim = queries.shape[1] // n_heads

    def attend_one_head(packed):
        head_index, factor = packed
        scores = inner(
            head_cols(queries, head_index, head_dim), head_cols(key_rows, head_index, head_dim)
        ) * (factor / math.sqrt(head_dim))
        row_top = jnp.max(scores, axis=1, keepdims=True)
        exp_scores = jnp.exp(scores - row_top)
        weights = (exp_scores / jnp.sum(exp_scores, axis=1, keepdims=True)).astype(jnp.bfloat16)
        return jnp.dot(
            weights, head_cols(val_rows, head_index, head_dim), preferred_element_type=jnp.float32
        )

    results = lax.map(attend_one_head, (jnp.arange(n_heads, dtype=jnp.int32), factors))
    return results.transpose(1, 0, 2).reshape(queries.shape).astype(jnp.bfloat16)


def read_parts(queries, key_rows, val_rows, factors, n_heads):
    head_dim = queries.shape[1] // n_heads

    def read_one_head(packed):
        head_index, factor = packed
        scores = inner(
            head_cols(queries, head_index, head_dim), head_cols(key_rows, head_index, head_dim)
        ) * (factor / math.sqrt(head_dim))
        row_top = jnp.max(scores, axis=1)
        exp_scores = jnp.exp(scores - row_top[:, None])
        totals = jnp.sum(exp_scores, axis=1)
        summed = jnp.dot(
            exp_scores.astype(jnp.bfloat16),
            head_cols(val_rows, head_index, head_dim),
            preferred_element_type=jnp.float32,
        )
        return (summed.astype(jnp.bfloat16), row_top, totals)

    return lax.map(read_one_head, (jnp.arange(n_heads, dtype=jnp.int32), factors))


def combine_parts(got_parts, got_tops, got_totals):
    row_best = jnp.max(got_tops, axis=0)
    rescale = jnp.exp(got_tops - row_best[None])
    summed = jnp.sum(got_parts.astype(jnp.float32) * rescale[..., None], axis=0)
    return summed / jnp.sum(got_totals * rescale, axis=0)[..., None]


def shards(tokens, latents, read_weights, later_weights, head_scale):
    own_rows = latents.shape[0]
    width = tokens.shape[1]
    read_full, later_full, lat_stack = (
        lax.all_gather(read_weights, "seq", axis=1, tiled=True),
        lax.all_gather(later_weights, "seq", axis=1, tiled=True),
        lax.all_gather(latents[None], "seq", axis=1, tiled=True),
    )
    tok_normed = norm_rows(tokens).astype(jnp.bfloat16)
    read_q = head_norm(project(norm_rows(lat_stack[0]).astype(jnp.bfloat16), read_full[0]), HEADS)
    read_k = head_norm(project(tok_normed, read_full[1]), HEADS)
    read_v = project(tok_normed, read_full[2]).astype(jnp.bfloat16)
    partials, row_tops, totals = read_parts(read_q, read_k, read_v, head_scale[0], HEADS)
    got_parts = lax.all_to_all(partials[None], "seq", split_axis=2, concat_axis=0, tiled=True)
    got_tops, got_totals = (
        lax.all_to_all(row_tops[None], "seq", split_axis=2, concat_axis=0, tiled=True),
        lax.all_to_all(totals[None], "seq", split_axis=2, concat_axis=0, tiled=True),
    )
    read_mixed = combine_parts(got_parts, got_tops, got_totals)
    read_mix = read_mixed.transpose(1, 0, 2).reshape(own_rows, width).astype(jnp.bfloat16)
    lat_one = latents.astype(jnp.float32) + project(read_mix, read_full[3])
    self_normed = norm_rows(lat_one).astype(jnp.bfloat16)
    self_q = head_norm(project(self_normed, later_full[0]), HEADS)
    self_k = head_norm(project(self_normed, later_full[1]), HEADS)
    self_v = project(self_normed, later_full[2]).astype(jnp.bfloat16)
    all_k, all_v = (
        lax.all_gather(self_k, "seq", axis=0, tiled=True),
        lax.all_gather(self_v, "seq", axis=0, tiled=True),
    )
    latents_out = lat_one + project(
        attend(self_q, all_k, all_v, head_scale[1], HEADS), later_full[3]
    )
    write_in = lax.all_gather(
        norm_rows(latents_out).astype(jnp.bfloat16), "seq", axis=0, tiled=True
    )
    write_q = head_norm(project(tok_normed, later_full[4]), HEADS)
    write_k = head_norm(project(write_in, later_full[5]), HEADS)
    write_v = project(write_in, later_full[6]).astype(jnp.bfloat16)
    tokens_out = (
        tokens.astype(jnp.float32)
        + project(attend(write_q, write_k, write_v, head_scale[2], HEADS), later_full[7])
    ).astype(jnp.bfloat16)
    return (tokens_out, latents_out)


def solution(mesh):
    placed = (
        P(("vid", "seq"), None),
        P(("vid", "seq"), None),
        P(None, "seq", None),
        P(None, "seq", None),
        P(),
    )
    return jax.shard_map(
        shards,
        mesh=mesh,
        in_specs=placed,
        out_specs=(P(("vid", "seq"), None), P(("vid", "seq"), None)),
        check_vma=False,
    )
```

profile of v0, /device:TPU:1, one launch (start us, length us, event | category | flops | bytes accessed | tf_op | source)
XLA Modules:
  0.0 380.3 jit_solution(12573883617736910417)
XLA Ops:
  8.7 11.7 %all-gather = bf16[512,768]{1,0:T(8,128)(2,1)S(1)} all-gather(bf16[64,768]{1,0:T(8,128)(2,1)S(1)} %copy-done.10), channel_id=2, replica_groups=mesh['seq'=8,'vid'=4] {'seq'}, dimensions={0}, use_global_device_ids=true | all-gather | bytes 884736 | tf_op jit(solution)/shard_map/all_gather | solution.py:92
  21.1 30.1 %all-gather.6.cloned.1.call-done = bf16[4,768,768]{2,1,0:T(8,128)(2,1)} async-done(((bf16[4,96,768]{2,1,0:T(8,128)(2,1)}), bf16[4,768,768]{2,1,0:T(8,128)(2,1)}) %all-gather.6.cloned.1.call-update) | async-done | bytes 4718608 | tf_op jit(solution)/shard_map/all_gather | solution.py:90
  51.2 1.8 slice_bitcast_fusion.15
  53.0 1.5 copy.35
  56.8 1.6 multiply_reduce_fusion.2
  58.6 1.6 multiply_convert_fusion
  60.3 4.0 %convolution_convert_fusion.1 = bf16[1024,768]{1,0:T(8,128)(2,1)} fusion(bf16[4,768,768]{2,1,0:T(8,128)(2,1)} %all-gather.6.cloned.1.call-done, bf16[1024,768]{1,0:T(8,128)(2,1)S(1)} %copy-done.3, f32[1024]{0:T(1024)S(1)} %add_rsqrt_fusion.6), kind=kOutput, calls=%fused_computation.56 | convolution fusion | flops 1211105280 | bytes 4329472 | tf_op jit(solution)/shard_map/dot_general | solution.py:26
  64.3 77.8 %while.34 = (s32[]{:T(128)}, bf16[12,512,64]{1,2,0:T(8,128)(2,1)}, f32[12,512]{1,0:T(8,128)S(1)}, f32[12,512]{1,0:T(8,128)S(1)}, s32[12]{0:T(128)S(1)}, /*index=...) while((s32[]{:T(128)}, bf16[12,512,64]{1,2,0:T(8,128)(2,1)}, ...), condition=%wide.region_8.9_spmd, body=%wide.region_5.8_spmd.sunk | while | flops 138443776 | bytes 6834919 | solution.py:76
  68.5 2.2 fusion.91
  75.0 2.2 fusion.91
  79.5 1.5 multiply_reduce_fusion.12
  81.5 2.2 fusion.91
  88.0 2.2 fusion.91
  94.5 2.2 fusion.91
  101.0 2.2 fusion.91
  107.5 2.2 fusion.91
  113.9 2.2 fusion.91
  120.4 2.2 fusion.91
  126.9 2.2 fusion.91
  133.4 2.2 fusion.91
  137.9 1.5 multiply_reduce_fusion.12
  139.9 2.2 fusion.91
  145.0 3.5 all-to-all-start.1
  150.9 2.0 copy.38
  152.9 4.2 %all-to-all-start.2 = ((f32[8,1,768]{2,1,0:T(1,128)}), f32[8,1,768]{2,1,0:T(1,128)S(1)}, u32[]{:S(2)}, u32[]{:S(2)}) async-start(f32[8,1,768]{2,1,0:T(1,128)} %reshape.165), calls=%async_computation.2 | async-start | bytes 49152 | tf_op jit(solution)/shard_map/all_to_all | solution.py:102
  157.1 1.7 bitcast_bitcast_fusion
  158.8 4.3 %reshape.161 = bf16[8,2,24576]{2,1,0:T(2,128)(2,1)} reshape(bf16[512,1,12,64]{3,2,1,0:T(8,128)(2,1)} %bitcast_bitcast_fusion) | data formatting | bytes 1572864
  163.1 4.2 %all-to-all-start = ((bf16[8,2,24576]{2,1,0:T(2,128)(2,1)}), bf16[8,2,24576]{2,1,0:T(2,128)(2,1)S(1)}, u32[]{:S(2)}, u32[]{:S(2)}) async-start(bf16[8,2,24576]{2,1,0:T(2,128)(2,1)} %reshape.161), calls=%async_computation | async-start | bytes 1572864 | tf_op jit(solution)/shard_map/all_to_all | solution.py:99
  170.1 6.3 %all-to-all-done = bf16[8,2,24576]{2,1,0:T(2,128)(2,1)S(1)} async-done(((bf16[8,2,24576]{2,1,0:T(2,128)(2,1)}), bf16[8,2,24576]{2,1,0:T(2,128)(2,1)S(1)}, u32[]{:S(2)}, u32[]{:S(2)}) %all-to-all-start) | async-done | bytes 786464 | tf_op jit(solution)/shard_map/all_to_all | solution.py:99
  176.4 2.2 reshape.162
  178.6 3.2 copy.39
  182.8 1.7 multiply_reduce_fusion.9
  186.0 3.7 slice_bitcast_fusion.9
  189.6 2.4 copy.47
  192.0 1.8 multiply_reduce_fusion.6
  194.5 1.7 copy.48
  196.2 14.6 %all_gather.21 = bf16[512,768]{1,0:T(8,128)(2,1)} all-gather(bf16[64,768]{1,0:T(8,128)(2,1)} %copy.48), channel_id=1, replica_groups=mesh['seq'=8,'vid'=4] {'seq'}, dimensions={0}, use_global_device_ids=true | all-gather | bytes 884736 | tf_op jit(solution)/shard_map/all_gather | solution.py:112
  210.8 1.7 fusion.47
  212.5 10.8 %all_gather.22 = bf16[512,768]{1,0:T(8,128)(2,1)} all-gather(bf16[64,768]{1,0:T(8,128)(2,1)S(1)} %fusion.47), channel_id=1, replica_groups=mesh['seq'=8,'vid'=4] {'seq'}, dimensions={0}, use_global_device_ids=true | all-gather | bytes 884736 | tf_op jit(solution)/shard_map/all_gather | solution.py:113
  224.8 1.8 multiply_reduce_fusion.7
  226.7 61.7 %while.35 = (s32[]{:T(128)}, bf16[12,64,64]{2,1,0:T(8,128)(2,1)S(1)}, s32[12]{0:T(128)S(1)}, bf16[64,768]{0,1:T(8,128)(2,1)S(1)}, bf16[512,768]{1,0:T(8,128)(2,1...) while((s32[]{:T(128)}, ...), condition=%wide.region_18.19_spmd, body=%wide.region_15.18_spmd.sunk | while | flops 8617863 | bytes 708555 | solution.py:54
  288.8 1.7 multiply_reduce_fusion.8
  290.6 11.1 %all_gather.23 = bf16[512,768]{1,0:T(8,128)(2,1)} all-gather(bf16[64,768]{1,0:T(8,128)(2,1)S(1)} %multiply_convert_fusion.6), channel_id=1, replica_groups=mesh['seq'=8,'vid'=4] {'seq'}, dimensions={0}, use_global_device_ids=true | all-gather | bytes 884736 | tf_op jit(solution)/shard_map/all_gather | solution.py:118
  302.4 3.1 multiply_reduce_fusion.4
  307.0 2.9 multiply_reduce_fusion.3
  311.3 2.0 convolution_convert_fusion.2
  313.4 55.2 %while.36 = (s32[]{:T(128)}, bf16[12,1024,64]{1,2,0:T(8,128)(2,1)}, s32[12]{0:T(128)S(1)}, bf16[1024,768]{0,1:T(8,128)(2,1)S(1)}, bf16[512,768]{0,1:T(8,128)(2,1...) while((s32[]{:T(128)}, bf16[12,1024,64]{1,2,0:T(8,128)(2,1)}, ...), condition=%wide.region_24.25_spmd, body=%wide.region_21.24_spmd.sunk | while | flops 138934272 | bytes 6904019 | solution.py:54
  368.6 4.8 %fusion.34 = bf16[1024,768]{1,0:T(8,128)(2,1)} fusion(bf16[1024,768]{1,0:T(8,128)(2,1)} %param.11, bf16[1024,768]{0,1:T(8,128)(2,1)} %bitcast.67, bf16[8,768,768]{2,1,0:T(8,128)(2,1)} %all-gather.4.cloned.1.call-done), kind=kOutput, calls=%fused_computation.47 | convolution fusion | flops 1210318848 | bytes 5898240 | tf_op jit(solution)/shard_map/dot_general | solution.py:26
  (275 shorter events, 141.3 us)
Async XLA Ops:
  7.2 1.5 copy-start.10
  7.2 44.0 %all-gather.6.cloned.1.call-start = ((), (), s32[]{:S(2)}) async-start(), calls=%async_computation.4 | async-start | bytes 5308416 | tf_op jit(solution)/shard_map/all_gather | solution.py:90
  7.9 12.8 %copy-start.2 = (bf16[1024,768]{1,0:T(8,128)(2,1)S(1)}, bf16[1024,768]{1,0:T(8,128)(2,1)}, u32[]{:S(2)}) copy-start(bf16[1024,768]{1,0:T(8,128)(2,1)} %param.11) | copy-start | bytes 4718596
  7.9 178.0 %all-gather.4.cloned.1.call-start = ((), (), s32[]{:S(2)}) async-start(), calls=%async_computation.3 | async-start | bytes 10616832 | tf_op jit(solution)/shard_map/all_gather | solution.py:91
  8.7 12.4 %copy-start.12 = (f32[3,12]{1,0:T(4,128)S(1)}, f32[3,12]{1,0:T(4,128)}, u32[]{:S(2)}) copy-start(f32[3,12]{1,0:T(4,128)} %param.15) | copy-start | bytes 436
  55.1 1.4 copy-start.3
  55.1 1.7 copy-start.6
  142.1 8.7 %copy-start.9 = (bf16[12,512,64]{1,2,0:T(8,128)(2,1)S(1)}, bf16[12,512,64]{1,2,0:T(8,128)(2,1)}, u32[]{:S(2)}) copy-start(bf16[12,512,64]{1,2,0:T(8,128)(2,1)} %get-tuple-element.125) | copy-start | bytes 2359300
  145.0 7.8 %all-to-all-start.1 = ((f32[8,1,768]{2,1,0:T(1,128)}), f32[8,1,768]{2,1,0:T(1,128)S(1)}, u32[]{:S(2)}, u32[]{:S(2)}) async-start(f32[8,1,768]{2,1,0:T(1,128)} %reshape.163), calls=%async_computation.1 | async-start | bytes 49152 | tf_op jit(solution)/shard_map/all_to_all | solution.py:101
  152.9 10.2 %all-to-all-start.2 = ((f32[8,1,768]{2,1,0:T(1,128)}), f32[8,1,768]{2,1,0:T(1,128)S(1)}, u32[]{:S(2)}, u32[]{:S(2)}) async-start(f32[8,1,768]{2,1,0:T(1,128)} %reshape.165), calls=%async_computation.2 | async-start | bytes 49152 | tf_op jit(solution)/shard_map/all_to_all | solution.py:102
  163.1 13.3 %all-to-all-start = ((bf16[8,2,24576]{2,1,0:T(2,128)(2,1)}), bf16[8,2,24576]{2,1,0:T(2,128)(2,1)S(1)}, u32[]{:S(2)}, u32[]{:S(2)}) async-start(bf16[8,2,24576]{2,1,0:T(2,128)(2,1)} %reshape.161), calls=%async_computation | async-start | bytes 1572864 | tf_op jit(solution)/shard_map/all_to_all | solution.py:99
  184.6 0.7 copy-start
  224.8 1.9 copy-start.11
  226.7 62.1 %copy-start.1 = (f32[64,768]{1,0:T(8,128)S(1)}, f32[64,768]{1,0:T(8,128)}, u32[]{:S(2)}) copy-start(f32[64,768]{1,0:T(8,128)} %copy-done) | copy-start | bytes 589828
  290.5 11.3 %copy-start.7 = (f32[64,768]{1,0:T(8,128)}, f32[64,768]{1,0:T(8,128)S(1)}, u32[]{:S(2)}) copy-start(f32[64,768]{1,0:T(8,128)S(1)} %get-tuple-element.275) | copy-start | bytes 589828
  305.5 1.5 copy-start.4
  307.0 3.0 copy-start.5
  310.2 1.1 copy-start.8
Sparse Core Ops, SparseCore 0:
  9.9 41.2 all-gather.5
  53.1 58.6 all-gather.3
where the time goes:
time: 383 us; the launch traced here: 380 us
  matrix products  122 us (32%)
  local copies, waits for them, and re-layouts  77.2 us (20%)
  blocking collectives  48.4 us (13%)
  loops' own time  45.6 us (12%)
  waiting for transfers between devices  37.8 us (10%)
  other arithmetic  23 us (6%)
  between operations  14.5 us (4%)
  starting transfers between devices  12.1 us (3%)
    dynamic_slice x72, local copies, waits for them, and re-layouts, read_parts(): lax.map(read_one_head, (jnp.arange(n_heads, dtype=jnp.int32), factors))  41.5 us
    dot_general x36, matrix products, inner(): lax.dot_general(left, right, (((1,), (1,)), ((), ())), preferred_element_...  38.4 us
    another operation x2, loops' own time, attend(): lax.map(attend_one_head, (jnp.arange(n_heads, dtype=jnp.int32), factors))  31.9 us
    all_gather x1, waiting for transfers between devices, shards(): lax.all_gather(read_weights, 'seq', axis=1, tiled=True)  30.1 us
    dot_general x24, matrix products, attend_one_head(): jnp.dot(weights, head_cols(val_rows, head_index, head_dim), preferred_ele...  29.1 us
    dot_general x12, matrix products, project(): return jnp.dot(inputs, weight, preferred_element_type=jnp.float32)  28.1 us
    dot_general x12, matrix products, read_one_head(): jnp.dot(exp_scores.astype(jnp.bfloat16), head_cols(val_rows, head_index,...  26.2 us
    all_gather x1, blocking collectives, shards(): lax.all_gather(self_k, 'seq', axis=0, tiled=True)  14.6 us
  transfers between devices with their start and end apart: 5, of which 2 were waited for; matrix products, arithmetic and copies ran while one was open for 27% of the time, Pallas kernels for 0%

commit v1 on v0

v1 whole, which is shorter than its diff:
```python
import functools
import math

import jax
import jax.numpy as jnp
from jax import lax
from jax.experimental import pallas as pl
from jax.experimental.pallas import tpu as pltpu
from jax.sharding import PartitionSpec as P

HEADS = 12
LANES = 128
epsilon = 1e-06
LOG2E = math.log2(math.e)
BF16 = jnp.bfloat16
F32 = jnp.float32


def rms(values):
    return values * lax.rsqrt(jnp.mean(values * values, axis=-1, keepdims=True) + epsilon)


def dot(left, right):
    return jnp.dot(left, right, preferred_element_type=F32)


def inner(left, right):
    return lax.dot_general(left, right, (((1,), (1,)), ((), ())), preferred_element_type=F32)


def group_matrix(head_dim):
    size = 2 * LANES
    row = lax.broadcasted_iota(jnp.int32, (size, size), 0) // head_dim
    col = lax.broadcasted_iota(jnp.int32, (size, size), 1) // head_dim
    return jnp.where(row == col, 1.0 / head_dim, 0.0).astype(BF16)


def head_norm(values, group):
    size = group.shape[0]
    parts = []
    for start in range(0, values.shape[1], size):
        block = values[:, start : start + size]
        square = block * block
        high = square.astype(BF16)
        low = (square - high.astype(F32)).astype(BF16)
        mean = dot(high, group) + dot(low, group)
        parts.append((block * lax.rsqrt(mean + epsilon)).astype(BF16))
    return jnp.concatenate(parts, axis=1)


def by_rows(rows, chunk, body):
    chunk = min(chunk, rows)

    def step(index, carry):
        body(pl.ds(pl.multiple_of(index * chunk, chunk), chunk))
        return carry

    lax.fori_loop(0, rows // chunk, step, 0)


def half_masks(head_dim):
    lane = lax.broadcasted_iota(jnp.int32, (1, LANES), 1) // head_dim
    return [(lane == part).astype(F32).astype(BF16) for part in range(LANES // head_dim)]


def merge_halves(parts, head_dim):
    lane = lax.broadcasted_iota(jnp.int32, parts[0].shape, 1) // head_dim
    result = parts[0]
    for part in range(1, len(parts)):
        result = jnp.where(lane == part, parts[part], result)
    return result


def attention(q_ref, k_ref, v_ref, scale_ref, which, out_ref, stats_ref, chunk):
    rows, width = q_ref.shape
    head_dim = width // HEADS
    per_block = LANES // head_dim
    chunk = min(chunk, rows)
    n_chunks = rows // chunk
    masks = half_masks(head_dim)
    root = 1.0 / math.sqrt(head_dim)

    def step(index, carry):
        block = index // n_chunks
        part = index % n_chunks
        cols = pl.ds(pl.multiple_of(block * LANES, LANES), LANES)
        here = pl.ds(pl.multiple_of(part * chunk, chunk), chunk)
        q = q_ref[here, cols]
        k = k_ref[:, cols]
        v = v_ref[:, cols]
        results = []
        for half in range(per_block):
            head = block * per_block + half
            factor = scale_ref[which, head] * root
            scores = inner(q * masks[half], k)
            top = jnp.max(scores, axis=1, keepdims=True)
            exp_scores = jnp.exp2((scores - top) * (factor * LOG2E))
            total = jnp.sum(exp_scores, axis=1, keepdims=True)
            if stats_ref is None:
                weights = (exp_scores * (1.0 / total)).astype(BF16)
            else:
                weights = exp_scores.astype(BF16)
                lane = lax.broadcasted_iota(jnp.int32, (chunk, LANES), 1)
                old = stats_ref[here, :]
                old = jnp.where(lane == head, top * factor, old)
                stats_ref[here, :] = jnp.where(lane == head + LANES // 2, total, old)
            results.append(dot(weights, v))
        out_ref[here, cols] = merge_halves(results, head_dim).astype(BF16)
        return carry

    lax.fori_loop(0, (width // LANES) * n_chunks, step, 0)


def read_body(tok_ref, lat_ref, w_ref, scale_ref, parts_ref, stats_ref, q_ref, k_ref, v_ref):
    group = group_matrix(tok_ref.shape[1] // HEADS)

    def latent_rows(here):
        normed = rms(lat_ref[here, :].astype(F32)).astype(BF16)
        q_ref[here, :] = head_norm(dot(normed, w_ref[0]), group)

    def token_rows(here):
        normed = rms(tok_ref[here, :].astype(F32)).astype(BF16)
        k_ref[here, :] = head_norm(dot(normed, w_ref[1]), group)
        v_ref[here, :] = dot(normed, w_ref[2]).astype(BF16)

    by_rows(lat_ref.shape[0], 256, latent_rows)
    by_rows(tok_ref.shape[0], 256, token_rows)
    attention(q_ref, k_ref, v_ref, scale_ref, 0, parts_ref, stats_ref, 256)


def combine_body(got_ref, stats_ref, lat_ref, out_w_ref, w_ref, one_ref, q_ref, kv_ref):
    count, rows, width = got_ref.shape
    head_dim = width // HEADS
    group = group_matrix(head_dim)
    per_block = LANES // head_dim
    stats = [stats_ref[b] for b in range(count)]
    best = functools.reduce(jnp.maximum, stats)
    rescale = [jnp.exp(item - best) for item in stats]
    half = LANES // 2
    bottom = sum(rescale[b][:, :half] * stats[b][:, half:] for b in range(count))
    inverse = 1.0 / bottom
    mixed = []
    for block in range(width // LANES):
        cols = slice(block * LANES, block * LANES + LANES)
        total = jnp.zeros((rows, LANES), F32)
        heads = range(block * per_block, block * per_block + per_block)

        def spread(values):
            return merge_halves(
                [jnp.broadcast_to(values[:, h : h + 1], (rows, LANES)) for h in heads], head_dim
            )

        for b in range(count):
            total += got_ref[b, :, cols].astype(F32) * spread(rescale[b])
        mixed.append((total * spread(inverse)).astype(BF16))
    read_mix = jnp.concatenate(mixed, axis=1)
    lat_one = lat_ref[...].astype(F32) + dot(read_mix, out_w_ref[...])
    one_ref[...] = lat_one
    normed = rms(lat_one).astype(BF16)
    q_ref[...] = head_norm(dot(normed, w_ref[0]), group)
    kv_ref[:, :width] = head_norm(dot(normed, w_ref[1]), group)
    kv_ref[:, width:] = dot(normed, w_ref[2]).astype(BF16)


def self_body(one_ref, q_ref, kv_ref, w_ref, scale_ref, out_ref, in_ref, mix_ref):
    width = one_ref.shape[1]
    attention(
        q_ref, kv_ref.at[:, :width], kv_ref.at[:, width:], scale_ref, 1, mix_ref, None, 64
    )
    latents_out = one_ref[...] + dot(mix_ref[...], w_ref[...])
    out_ref[...] = latents_out
    in_ref[...] = rms(latents_out).astype(BF16)


def write_body(tok_ref, in_ref, w_ref, scale_ref, out_ref, q_ref, k_ref, v_ref, mix_ref):
    group = group_matrix(tok_ref.shape[1] // HEADS)

    def latent_rows(here):
        k_ref[here, :] = head_norm(dot(in_ref[here, :], w_ref[1]), group)
        v_ref[here, :] = dot(in_ref[here, :], w_ref[2]).astype(BF16)

    def token_rows(here):
        normed = rms(tok_ref[here, :].astype(F32)).astype(BF16)
        q_ref[here, :] = head_norm(dot(normed, w_ref[0]), group)

    def out_rows(here):
        out_ref[here, :] = (
            tok_ref[here, :].astype(F32) + dot(mix_ref[here, :], w_ref[3])
        ).astype(out_ref.dtype)

    by_rows(in_ref.shape[0], 256, latent_rows)
    by_rows(tok_ref.shape[0], 256, token_rows)
    attention(q_ref, k_ref, v_ref, scale_ref, 2, mix_ref, None, 256)
    by_rows(tok_ref.shape[0], 256, out_rows)


VM = pl.BlockSpec(memory_space=pltpu.VMEM)
SM = pl.BlockSpec(memory_space=pltpu.SMEM)


def call(body, in_specs, outs, scratch, *args):
    return pl.pallas_call(
        body,
        out_shape=[jax.ShapeDtypeStruct(shape, dtype) for shape, dtype in outs],
        in_specs=in_specs,
        out_specs=[VM] * len(outs),
        scratch_shapes=[pltpu.VMEM(shape, dtype) for shape, dtype in scratch],
        compiler_params=pltpu.CompilerParams(vmem_limit_bytes=56 * 1024 * 1024),
    )(*args)


def gathered(count, tokens, latents, read_weights, later_weights, head_scale):
    own, width = latents.shape
    rows = own * count
    slab = tokens.shape[0]
    read_full = lax.all_gather(read_weights, "seq", axis=1, tiled=True)
    later_full = lax.all_gather(later_weights, "seq", axis=1, tiled=True)
    lat_all = lax.all_gather(latents, "seq", axis=0, tiled=True)
    parts, stats = call(
        read_body,
        [VM, VM, VM, SM],
        [((rows, width), BF16), ((rows, LANES), F32)],
        [((rows, width), BF16), ((slab, width), BF16), ((slab, width), BF16)],
        tokens, lat_all, read_full[:3], head_scale,
    )
    got_parts = lax.all_to_all(
        parts.reshape(count, own, width), "seq", split_axis=0, concat_axis=0, tiled=True
    )
    got_stats = lax.all_to_all(
        stats.reshape(count, own, LANES), "seq", split_axis=0, concat_axis=0, tiled=True
    )
    lat_one, self_q, self_kv = call(
        combine_body,
        [VM] * 5,
        [((own, width), F32), ((own, width), BF16), ((own, 2 * width), BF16)],
        [],
        got_parts, got_stats, latents, read_full[3], later_full[:3],
    )
    all_kv = lax.all_gather(self_kv, "seq", axis=0, tiled=True)
    latents_out, write_in = call(
        self_body,
        [VM, VM, VM, VM, SM],
        [((own, width), F32), ((own, width), BF16)],
        [((own, width), BF16)],
        lat_one, self_q, all_kv, later_full[3], head_scale,
    )
    write_all = lax.all_gather(write_in, "seq", axis=0, tiled=True)
    (tokens_out,) = call(
        write_body,
        [VM, VM, VM, SM],
        [((slab, width), BF16)],
        [((slab, width), BF16), ((rows, width), BF16), ((rows, width), BF16), ((slab, width), BF16)],
        tokens, write_all, later_full[4:], head_scale,
    )
    return tokens_out, latents_out


def solution(mesh):
    placed = (
        P(("vid", "seq"), None),
        P(("vid", "seq"), None),
        P(None, "seq", None),
        P(None, "seq", None),
        P(),
    )
    return jax.shard_map(
        functools.partial(gathered, mesh.shape["seq"]),
        mesh=mesh,
        in_specs=placed,
        out_specs=(P(("vid", "seq"), None), P(("vid", "seq"), None)),
        check_vma=False,
    )
```

time: 383 us -> 222 us (0.58)
  matrix products: 122 us -> 0 us
  Pallas kernels: 0 us -> 73.2 us
  local copies, waits for them, and re-layouts: 77.2 us -> 18.6 us
  loops' own time: 45.6 us -> 0 us
  waiting for transfers between devices: 37.8 us -> 73.7 us
  other arithmetic: 23 us -> 0 us
  blocking collectives: 48.4 us -> 35.5 us
  starting transfers between devices: 12.1 us -> 6.82 us
    dot_general x84 -> x0, matrix products: 122 us -> none  [the longest x36 38.4 us: inner(): lax.dot_general(left, right, (((1,), (1,)), ((), ())), preferred_element_...]
    pallas_call x0 -> x4, Pallas kernels: none -> 73.2 us  [call(): pl.pallas_call(body, out_shape=[jax.ShapeDtypeStruct(shape, dtype) for sh...]
    another operation x3 -> x0, loops' own time: 45.6 us -> none  [the longest x2 31.9 us: attend(): lax.map(attend_one_head, (jnp.arange(n_heads, dtype=jnp.int32), factors))]
    all_gather x2 -> x3, waiting for transfers between devices: 30.1 us -> 72.3 us  [the longest x1 29.7 us: gathered(): read_full = lax.all_gather(read_weights, 'seq', axis=1, tiled=True)]
    dynamic_slice x72 -> x0, local copies, waits for them, and re-layouts: 41.5 us -> none  [read_parts(): lax.map(read_one_head, (jnp.arange(n_heads, dtype=jnp.int32), factors))]
    all_gather x4 -> x2, blocking collectives: 48.4 us -> 24.4 us  [the longest x1 12.8 us: gathered(): lat_all = lax.all_gather(latents, 'seq', axis=0, tiled=True)]
    reduce_sum x40 -> x0, other arithmetic: 14.5 us -> none  [the longest x24 6.83 us: attend_one_head(): jnp.sum(exp_scores, axis=1, keepdims=True)]
    dot_general x8 -> x0, local copies, waits for them, and re-layouts: 13.4 us -> none  [project(): return jnp.dot(inputs, weight, preferred_element_type=jnp.float32)]
  transfers between devices with their start and end apart: 5 -> 4, of which waited for: 2 -> 3; matrix products, arithmetic and copies ran while one was open for 27% -> 8% of each run, Pallas kernels for 0% -> 11%
where the time goes in v1:
time: 222 us
  waiting for transfers between devices  73.7 us (33%)
  Pallas kernels  73.2 us (33%)
  blocking collectives  35.5 us (16%)
  local copies, waits for them, and re-layouts  18.6 us (8%)
  between operations  13.8 us (6%)
  starting transfers between devices  6.82 us (3%)
    pallas_call x4, Pallas kernels, call(): pl.pallas_call(body, out_shape=[jax.ShapeDtypeStruct(shape, dtype) for sh...  73.2 us
    all_gather x1, waiting for transfers between devices, gathered(): read_full = lax.all_gather(read_weights, 'seq', axis=1, tiled=True)  29.7 us
    all_gather x1, waiting for transfers between devices, gathered(): later_full = lax.all_gather(later_weights, 'seq', axis=1, tiled=True)  24.1 us
    all_gather x1, waiting for transfers between devices, gathered(): all_kv = lax.all_gather(self_kv, 'seq', axis=0, tiled=True)  18.5 us
    all_gather x1, blocking collectives, gathered(): lat_all = lax.all_gather(latents, 'seq', axis=0, tiled=True)  12.8 us
    all_gather x1, blocking collectives, gathered(): write_all = lax.all_gather(write_in, 'seq', axis=0, tiled=True)  11.6 us
    all_to_all x1, blocking collectives, gathered(): lax.all_to_all(stats.reshape(count, own, LANES), 'seq', split_axis=0, con...  11.1 us
    all_to_all x1, starting transfers between devices, gathered(): lax.all_to_all(parts.reshape(count, own, width), 'seq', split_axis=0, con...  6.74 us
  transfers between devices with their start and end apart: 4, of which 3 were waited for; matrix products, arithmetic and copies ran while one was open for 8% of the time, Pallas kernels for 11%

profile of v1, /device:TPU:1, one launch (start us, length us, event | category | flops | bytes accessed | tf_op | source)
XLA Modules:
  0.0 221.5 jit_solution(14496742370362883036)
XLA Ops:
  7.2 0.0 copy-start.1
  7.2 0.0 all-gather.4.cloned.1.call-start
  7.2 0.7 all-gather.4.cloned.1.call-update
  7.9 0.0 all-gather.6.cloned.1.call-start
  8.0 0.7 all-gather.6.cloned.1.call-update
  8.7 0.0 copy-done.1
  8.7 12.8 %all_gather.15.lat_ref = bf16[512,768]{1,0:T(8,128)(2,1)} all-gather(bf16[64,768]{1,0:T(8,128)(2,1)S(1)} %copy-done.1), channel_id=1, replica_groups=mesh['seq'=8,'vid'=4] {'seq'}, dimensions={0}, use_global_device_ids=true | all-gather | bytes 884736 | tf_op jit(solution)/shard_map/all_gather | solution.py:218
  21.5 29.7 %all-gather.4.cloned.1.call-done = bf16[4,768,768]{2,1,0:T(8,128)(2,1)} async-done(((bf16[4,96,768]{2,1,0:T(8,128)(2,1)}), bf16[4,768,768]{2,1,0:T(8,128)(2,1)}) %all-gather.4.cloned.1.call-update) | async-done | bytes 4718608 | tf_op jit(solution)/shard_map/all_gather | solution.py:216
  51.2 4.0 %slice.20.w_ref = bf16[3,768,768]{2,1,0:T(8,128)(2,1)} slice(bf16[4,768,768]{2,1,0:T(8,128)(2,1)} %all-gather.4.cloned.1.call-done), slice={[0:3], [0:768], [0:768]} | slice | bytes 7077888 | tf_op jit(solution)/shard_map/slice | solution.py:224
  55.2 23.5 %shard_map.68 = (bf16[512,768]{1,0:T(8,128)(2,1)}, f32[512,128]{1,0:T(8,128)}) custom-call(bf16[1024,768]{1,0:T(8,128)(2,1)} %tok_ref.3, bf16[512,768]{1,0:T(8,128)(2,1)} %all_gather.15.lat_ref, bf16[3,768,768]{2,1,0:T(8,128)(2,1)} %slice.20.w_ref, f32[3,12]{1,0:T(4,128)} %scale_ref.5), custom_call_target="tpu_custom_call" | custom-call | tf_op jit(solution)/shard_map/pallas_call | solution.py:202
  78.7 11.1 %all_to_all.10.stats_ref = f32[8,64,128]{2,1,0:T(8,128)} all-to-all(f32[8,64,128]{2,1,0:T(8,128)} %bitcast.7), channel_id=1, replica_groups=mesh['seq'=8,'vid'=4] {'seq'}, dimensions={0} | all-to-all | bytes 524288 | tf_op jit(solution)/shard_map/all_to_all | solution.py:229
  89.8 6.7 %all-to-all-start = ((bf16[8,64,768]{2,1,0:T(8,128)(2,1)}), bf16[8,64,768]{2,1,0:T(8,128)(2,1)S(1)}, u32[]{:S(2)}, u32[]{:S(2)}) async-start(bf16[8,64,768]{2,1,0:T(8,128)(2,1)} %bitcast.6), calls=%async_computation | async-start | bytes 1572864 | tf_op jit(solution)/shard_map/all_to_all | solution.py:226
  96.5 0.0 all-gather.8.cloned.1.call-start
  96.5 2.4 %slice_bitcast_fusion.1.out_w_ref = bf16[768,768]{1,0:T(8,128)(2,1)} fusion(bf16[4,768,768]{2,1,0:T(8,128)(2,1)} %all-gather.4.cloned.1.call-done), kind=kLoop, calls=%fused_computation.1 | loop fusion | bytes 2359296 | tf_op jit(solution)/shard_map/squeeze | solution.py:237
  98.9 24.1 %all-gather.6.cloned.1.call-done = bf16[8,768,768]{2,1,0:T(8,128)(2,1)} async-done(((bf16[8,96,768]{2,1,0:T(8,128)(2,1)}), bf16[8,768,768]{2,1,0:T(8,128)(2,1)}) %all-gather.6.cloned.1.call-update) | async-done | bytes 9437200 | tf_op jit(solution)/shard_map/all_gather | solution.py:217
  123.1 4.0 %slice.22.w_ref = bf16[3,768,768]{2,1,0:T(8,128)(2,1)} slice(bf16[8,768,768]{2,1,0:T(8,128)(2,1)} %all-gather.6.cloned.1.call-done), slice={[0:3], [0:768], [0:768]} | slice | bytes 7077888 | tf_op jit(solution)/shard_map/slice | solution.py:237
  127.1 0.0 all-to-all-done.got_ref
  127.1 0.0 copy-start
  127.1 0.9 copy-done
  128.0 6.1 %shard_map.69 = (f32[64,768]{1,0:T(8,128)}, bf16[64,768]{1,0:T(8,128)(2,1)}, bf16[64,1536]{1,0:T(8,128)(2,1)}) custom-call(bf16[8,64,768]{2,1,0:T(8,128)(2,1)} %copy-done, f32[8,64,128]{2,1,0:T(8,128)} %all_to_all.10.stats_ref, bf16[64,768]{1,0:T(8,128)(2,1)} %lat_ref.1, bf16[768,768]{1,0:T(8,128)(2,1)} %slice_bitcast_fusion.1.out_w_ref, ...), custom_call_target="tpu_custom_call" | custom-call | tf_op jit(solution)/shard_map/pallas_call | solution.py:202
  134.1 0.0 all-gather.8.cloned.1.call-update
  134.2 4.9 %slice.24.w_ref = bf16[4,768,768]{2,1,0:T(8,128)(2,1)} slice(bf16[8,768,768]{2,1,0:T(8,128)(2,1)} %all-gather.6.cloned.1.call-done), slice={[4:8], [0:768], [0:768]} | slice | bytes 9437184 | tf_op jit(solution)/shard_map/slice | solution.py:253
  139.0 2.4 %slice_bitcast_fusion.w_ref = bf16[768,768]{1,0:T(8,128)(2,1)} fusion(bf16[8,768,768]{2,1,0:T(8,128)(2,1)} %all-gather.6.cloned.1.call-done), kind=kLoop, calls=%fused_computation | loop fusion | bytes 2359296 | tf_op jit(solution)/shard_map/squeeze | solution.py:245
  141.4 18.5 %all-gather.8.cloned.1.call-done.kv_ref = bf16[512,1536]{1,0:T(8,128)(2,1)} async-done(((bf16[64,1536]{1,0:T(8,128)(2,1)}), bf16[512,1536]{1,0:T(8,128)(2,1)}) %all-gather.8.cloned.1.call-update) | async-done | bytes 1572880 | tf_op jit(solution)/shard_map/all_gather | solution.py:239
  159.9 7.9 %shard_map.70 = (f32[64,768]{1,0:T(8,128)}, bf16[64,768]{1,0:T(8,128)(2,1)}) custom-call(f32[64,768]{1,0:T(8,128)} %get-tuple-element.11.one_ref, bf16[64,768]{1,0:T(8,128)(2,1)} %get-tuple-element.12.q_ref, bf16[512,1536]{1,0:T(8,128)(2,1)} %all-gather.8.cloned.1.call-done.kv_ref, bf16[768,768]{1,0:T(8,128)(2,1)} %slice_bitcast_fusion.w_ref, f32[3,12]{1,0:T(4,128)} %scale_ref.5), custom_call_target="tpu_custom_call" | custom-call | tf_op jit(solution)/shard_map/pallas_call | solution.py:202
  167.7 11.6 %all_gather.19.in_ref = bf16[512,768]{1,0:T(8,128)(2,1)} all-gather(bf16[64,768]{1,0:T(8,128)(2,1)} %get-tuple-element.14), channel_id=1, replica_groups=mesh['seq'=8,'vid'=4] {'seq'}, dimensions={0}, use_global_device_ids=true | all-gather | bytes 884736 | tf_op jit(solution)/shard_map/all_gather | solution.py:247
  179.3 35.7 %shard_map.71 = bf16[1024,768]{1,0:T(8,128)(2,1)} custom-call(bf16[1024,768]{1,0:T(8,128)(2,1)} %tok_ref.3, bf16[512,768]{1,0:T(8,128)(2,1)} %all_gather.19.in_ref, bf16[4,768,768]{2,1,0:T(8,128)(2,1)} %slice.24.w_ref, f32[3,12]{1,0:T(4,128)} %scale_ref.5), custom_call_target="tpu_custom_call" | custom-call | tf_op jit(solution)/shard_map/pallas_call | solution.py:202
Async XLA Ops:
  7.2 1.5 copy-start.1
  7.2 44.0 %all-gather.4.cloned.1.call-start = ((), (), s32[]{:S(2)}) async-start(), calls=%async_computation.2 | async-start | bytes 5308416 | tf_op jit(solution)/shard_map/all_gather | solution.py:216
  7.9 115.1 %all-gather.6.cloned.1.call-start = ((), (), s32[]{:S(2)}) async-start(), calls=%async_computation.3 | async-start | bytes 10616832 | tf_op jit(solution)/shard_map/all_gather | solution.py:217
  89.8 37.3 %all-to-all-start = ((bf16[8,64,768]{2,1,0:T(8,128)(2,1)}), bf16[8,64,768]{2,1,0:T(8,128)(2,1)S(1)}, u32[]{:S(2)}, u32[]{:S(2)}) async-start(bf16[8,64,768]{2,1,0:T(8,128)(2,1)} %bitcast.6), calls=%async_computation | async-start | bytes 1572864 | tf_op jit(solution)/shard_map/all_to_all | solution.py:226
  96.5 63.4 %all-gather.8.cloned.1.call-start = ((), (), s32[]{:S(2)}) async-start(), calls=%async_computation.4 | async-start | bytes 1769472 | tf_op jit(solution)/shard_map/all_gather | solution.py:239
  127.1 0.9 copy-start
Sparse Core Ops, SparseCore 0:
  9.9 41.2 all-gather.3
  53.1 69.9 all-gather.5
  134.3 25.5 all-gather.7

commit v2 on v1

--- a/solution.py
+++ b/solution.py
@@ -71,7 +71,7 @@
     return result
 
 
-def attention(q_ref, k_ref, v_ref, scale_ref, which, out_ref, stats_ref, chunk):
+def attention(q_ref, k_ref, v_ref, scale_ref, which, out_ref, stats_ref, chunk, hooks=None):
     rows, width = q_ref.shape
     head_dim = width // HEADS
     per_block = LANES // head_dim
@@ -81,6 +81,8 @@
     root = 1.0 / math.sqrt(head_dim)
 
     def step(index, carry):
+        for when, action in (hooks or {}).items():
+            pl.when(index == when)(action)
         block = index // n_chunks
         part = index % n_chunks
         cols = pl.ds(pl.multiple_of(block * LANES, LANES), LANES)
@@ -114,6 +116,8 @@
 def read_body(tok_ref, lat_ref, w_ref, scale_ref, parts_ref, stats_ref, q_ref, k_ref, v_ref):
     group = group_matrix(tok_ref.shape[1] // HEADS)
 
+    stats_ref[...] = jnp.zeros(stats_ref.shape, F32)
+
     def latent_rows(here):
         normed = rms(lat_ref[here, :].astype(F32)).astype(BF16)
         q_ref[here, :] = head_norm(dot(normed, w_ref[0]), group)
@@ -128,12 +132,12 @@
     attention(q_ref, k_ref, v_ref, scale_ref, 0, parts_ref, stats_ref, 256)
 
 
-def combine_body(got_ref, stats_ref, lat_ref, out_w_ref, w_ref, one_ref, q_ref, kv_ref):
-    count, rows, width = got_ref.shape
+def combine(got, stats, lat_ref, out_w_ref, w_refs, one_ref, q_ref, kv_ref):
+    count = len(got)
+    rows, width = got[0].shape
     head_dim = width // HEADS
     group = group_matrix(head_dim)
     per_block = LANES // head_dim
-    stats = [stats_ref[b] for b in range(count)]
     best = functools.reduce(jnp.maximum, stats)
     rescale = [jnp.exp(item - best) for item in stats]
     half = LANES // 2
@@ -151,15 +155,24 @@
             )
 
         for b in range(count):
-            total += got_ref[b, :, cols].astype(F32) * spread(rescale[b])
+            total += got[b][:, cols].astype(F32) * spread(rescale[b])
         mixed.append((total * spread(inverse)).astype(BF16))
     read_mix = jnp.concatenate(mixed, axis=1)
     lat_one = lat_ref[...].astype(F32) + dot(read_mix, out_w_ref[...])
     one_ref[...] = lat_one
     normed = rms(lat_one).astype(BF16)
-    q_ref[...] = head_norm(dot(normed, w_ref[0]), group)
-    kv_ref[:, :width] = head_norm(dot(normed, w_ref[1]), group)
-    kv_ref[:, width:] = dot(normed, w_ref[2]).astype(BF16)
+    q_ref[...] = head_norm(dot(normed, w_refs[0][...]), group)
+    kv_ref[:, :width] = head_norm(dot(normed, w_refs[1][...]), group)
+    kv_ref[:, width:] = dot(normed, w_refs[2][...]).astype(BF16)
+
+
+def combine_body(got_ref, stats_ref, lat_ref, out_w_ref, w_ref, one_ref, q_ref, kv_ref):
+    count = got_ref.shape[0]
+    combine(
+        [got_ref[b] for b in range(count)],
+        [stats_ref[b] for b in range(count)],
+        lat_ref, out_w_ref, [w_ref.at[i] for i in range(3)], one_ref, q_ref, kv_ref,
+    )
 
 
 def self_body(one_ref, q_ref, kv_ref, w_ref, scale_ref, out_ref, in_ref, mix_ref):
@@ -255,6 +268,310 @@
     return tokens_out, latents_out
 
 
+class Gather:
+    def __init__(self, source, place, rows, sems, item, spots):
+        send, recv = sems
+        me, core, along_x, along_y, diagonal = spots
+        half = rows // 2
+        self.done = set()
+
+        def copy(kind, src, dst, target):
+            return pltpu.make_async_remote_copy(
+                src_ref=src,
+                dst_ref=dst,
+                send_sem=send.at[item, kind],
+                recv_sem=recv.at[item, kind],
+                device_id={"seq": target},
+                device_id_type=pl.DeviceIdType.MESH,
+            )
+
+        def block(owner, start=0, size=rows):
+            return place(pl.ds(pl.multiple_of(owner * rows + start, half), size))
+
+        mine = source if source is not None else block(me)
+        self.first = [
+            copy(0, mine, block(me), along_x),
+            copy(1, mine, block(me), along_y),
+            copy(2, mine, block(me), core),
+        ]
+        self.relay = [
+            copy(3, block(along_x, 0, half), block(along_x, 0, half), along_y),
+            copy(4, block(along_y, half, half), block(along_y, half, half), along_x),
+            copy(5, block(along_x), block(along_x), core),
+            copy(6, block(along_y), block(along_y), core),
+        ]
+        self.last = [copy(7, block(diagonal), block(diagonal), core)]
+        self.local = None
+        if source is not None:
+            self.local = pltpu.make_async_copy(source, block(me), send.at[item, 8])
+
+    def start(self):
+        if "start" not in self.done:
+            self.done.add("start")
+            for copy in self.first:
+                copy.start()
+            if self.local is not None:
+                self.local.start()
+
+    def spread(self):
+        if "spread" not in self.done:
+            self.done.add("spread")
+            self.first[0].wait_recv()
+            self.relay[0].start()
+            self.relay[2].start()
+            self.first[1].wait_recv()
+            self.relay[1].start()
+            self.relay[3].start()
+
+    def close(self):
+        if "close" not in self.done:
+            self.done.add("close")
+            self.relay[0].wait_recv()
+            self.relay[1].wait_recv()
+            self.last[0].start()
+
+    def need(self):
+        self.spread()
+        self.close()
+        self.first[2].wait_recv()
+        self.relay[2].wait_recv()
+        self.relay[3].wait_recv()
+        self.last[0].wait_recv()
+        if self.local is not None:
+            self.local.wait()
+
+    def drain(self):
+        for copy in self.first + self.relay + self.last:
+            copy.wait_send()
+
+
+def whole_body(
+    count, tok_ref, lat_ref, rw_ref, lw_ref, scale_ref, out_ref, lat_out_ref,
+    w_ref, norm_ref, lat_all, q_ref, k_ref, v_ref, parts_ref, stats_ref,
+    got_ref, got_stats, one_ref, self_q, kv_ref, mix_small, in_ref,
+    wq_ref, wk_ref, wv_ref, mix_ref, send, recv, slab_send, slab_recv,
+):
+    me = lax.axis_index("seq")
+    core = me + 1 - 2 * (me % 2)
+    along_x = me + 2 - 4 * ((me // 2) % 2)
+    along_y = me + 4 - 8 * (me // 4)
+    diagonal = along_x + 4 - 8 * (me // 4)
+    spots = (me, core, along_x, along_y, diagonal)
+    own, width = lat_ref.shape
+    n_read = rw_ref.shape[0]
+    shard = rw_ref.shape[1]
+    group = group_matrix(width // HEADS)
+    sems = (send, recv)
+
+    barrier = pltpu.get_barrier_semaphore()
+    for step in range(1, count):
+        pl.semaphore_signal(
+            barrier, inc=1, device_id={"seq": (me + step) % count},
+            device_id_type=pl.DeviceIdType.MESH,
+        )
+    pl.semaphore_wait(barrier, count - 1)
+
+    def matrix(item, index):
+        source = rw_ref.at[index] if index < n_read else lw_ref.at[index - n_read]
+        return Gather(source, lambda rows: w_ref.at[index, rows], shard, sems, item, spots)
+
+    def array(item, source, ref):
+        return Gather(source, lambda rows: ref.at[rows], own, sems, item, spots)
+
+    r1, r2 = matrix(0, 1), matrix(1, 2)
+    lat = array(2, lat_ref, lat_all)
+    r0, l4, r3 = matrix(3, 0), matrix(4, n_read + 4), matrix(5, 3)
+    l0, l1, l2 = (matrix(6 + i, n_read + i) for i in range(3))
+    l3, l5, l6, l7 = (matrix(9 + i, n_read + j) for i, j in enumerate((3, 5, 6, 7)))
+    kv, into = array(13, None, kv_ref), array(14, None, in_ref)
+
+    r1.start()
+    r2.start()
+    lat.start()
+
+    def norm_rows(here):
+        norm_ref[here, :] = rms(tok_ref[here, :].astype(F32)).astype(BF16)
+
+    slab = tok_ref.shape[0]
+    by_rows(slab, 256, norm_rows)
+    stats_ref[...] = jnp.zeros(stats_ref.shape, F32)
+    r1.spread()
+    r0.start()
+    r2.spread()
+    r1.need()
+
+    def key_rows(here):
+        k_ref[here, :] = head_norm(dot(norm_ref[here, :], w_ref[1]), group)
+
+    by_rows(slab, 256, key_rows)
+    lat.spread()
+    l4.start()
+    r2.need()
+
+    def value_rows(here):
+        v_ref[here, :] = dot(norm_ref[here, :], w_ref[2]).astype(BF16)
+
+    by_rows(slab, 256, value_rows)
+    lat.close()
+    r0.spread()
+    r3.start()
+    lat.need()
+    r0.need()
+    l4.spread()
+    l0.start()
+
+    def query_rows(here):
+        normed = rms(lat_all[here, :].astype(F32)).astype(BF16)
+        q_ref[here, :] = head_norm(dot(normed, w_ref[0]), group)
+
+    by_rows(lat_all.shape[0], 256, query_rows)
+
+    def run(*actions):
+        def body():
+            for action in actions:
+                action()
+
+        return body
+
+    attention(
+        q_ref, k_ref, v_ref, scale_ref, 0, parts_ref, stats_ref, 256,
+        {
+            0: run(l4.close, r3.spread, l1.start),
+            3: run(r3.close, l0.spread, l2.start),
+            6: run(l0.close, l1.spread),
+            9: run(l1.close, l2.spread),
+        },
+    )
+    sums = []
+    for step in range(1, count):
+        target = (me + step) % count
+        rows = pl.ds(pl.multiple_of(target * own, own), own)
+        for kind, (src, dst) in enumerate(((parts_ref, got_ref), (stats_ref, got_stats))):
+            copy = pltpu.make_async_remote_copy(
+                src_ref=src.at[rows],
+                dst_ref=dst.at[step - 1],
+                send_sem=slab_send.at[step - 1, kind],
+                recv_sem=slab_recv.at[step - 1, kind],
+                device_id={"seq": target},
+                device_id_type=pl.DeviceIdType.MESH,
+            )
+            copy.start()
+            sums.append(copy)
+    l2.close()
+    l3.start()
+    l4.need()
+
+    def write_query_rows(here):
+        wq_ref[here, :] = head_norm(dot(norm_ref[here, :], w_ref[n_read + 4]), group)
+
+    by_rows(slab, 256, write_query_rows)
+    for item in (r3, l0, l1, l2):
+        item.need()
+    for copy in sums:
+        copy.wait_recv()
+    mine = pl.ds(pl.multiple_of(me * own, own), own)
+    combine(
+        [parts_ref[mine, :]] + [got_ref[b] for b in range(count - 1)],
+        [stats_ref[mine, :]] + [got_stats[b] for b in range(count - 1)],
+        lat_ref, w_ref.at[3], [w_ref.at[n_read + i] for i in range(3)],
+        one_ref, self_q, kv_ref.at[mine],
+    )
+    kv.start()
+    l3.spread()
+    l5.start()
+    l6.start()
+    l3.close()
+    kv.need()
+    attention(
+        self_q, kv_ref.at[:, :width], kv_ref.at[:, width:], scale_ref, 1, mix_small, None, own
+    )
+    l3.need()
+    latents_out = one_ref[...] + dot(mix_small[...], w_ref[n_read + 3])
+    lat_out_ref[...] = latents_out
+    in_ref[mine, :] = rms(latents_out).astype(BF16)
+    into.start()
+    l5.spread()
+    l6.spread()
+    l7.start()
+    into.spread()
+    l5.close()
+    l6.close()
+    into.need()
+    l5.need()
+
+    def write_key_rows(here):
+        wk_ref[here, :] = head_norm(dot(in_ref[here, :], w_ref[n_read + 5]), group)
+
+    def write_value_rows(here):
+        wv_ref[here, :] = dot(in_ref[here, :], w_ref[n_read + 6]).astype(BF16)
+
+    by_rows(lat_all.shape[0], 256, write_key_rows)
+    l6.need()
+    by_rows(lat_all.shape[0], 256, write_value_rows)
+    attention(
+        wq_ref, wk_ref, wv_ref, scale_ref, 2, mix_ref, None, 256,
+        {2: l7.spread, 6: l7.close},
+    )
+    l7.need()
+
+    def out_rows(here):
+        out_ref[here, :] = (
+            tok_ref[here, :].astype(F32) + dot(mix_ref[here, :], w_ref[n_read + 7])
+        ).astype(out_ref.dtype)
+
+    by_rows(slab, 256, out_rows)
+    for item in (r1, r2, lat, r0, l4, r3, l0, l1, l2, l3, l5, l6, l7, kv, into):
+        item.drain()
+    for copy in sums:
+        copy.wait_send()
+
+
+def cube(count, tokens, latents, read_weights, later_weights, head_scale):
+    own, width = latents.shape
+    rows = own * count
+    slab = tokens.shape[0]
+    matrices = read_weights.shape[0] + later_weights.shape[0]
+    vmem = lambda *shape: pltpu.VMEM(shape, BF16)
+    full = lambda *shape: pltpu.VMEM(shape, F32)
+    return pl.pallas_call(
+        functools.partial(whole_body, count),
+        out_shape=[
+            jax.ShapeDtypeStruct(tokens.shape, BF16),
+            jax.ShapeDtypeStruct(latents.shape, F32),
+        ],
+        in_specs=[VM, VM, pl.BlockSpec(memory_space=pl.ANY), pl.BlockSpec(memory_space=pl.ANY), SM],
+        out_specs=[VM, VM],
+        scratch_shapes=[
+            vmem(matrices, width, width),
+            vmem(slab, width),
+            vmem(rows, width),
+            vmem(rows, width),
+            vmem(slab, width),
+            vmem(slab, width),
+            vmem(rows, width),
+            full(rows, LANES),
+            vmem(count - 1, own, width),
+            full(count - 1, own, LANES),
+            full(own, width),
+            vmem(own, width),
+            vmem(rows, 2 * width),
+            vmem(own, width),
+            vmem(rows, width),
+            vmem(slab, width),
+            vmem(rows, width),
+            vmem(rows, width),
+            vmem(slab, width),
+            pltpu.SemaphoreType.DMA((matrices + 3, 9)),
+            pltpu.SemaphoreType.DMA((matrices + 3, 8)),
+            pltpu.SemaphoreType.DMA((count - 1, 2)),
+            pltpu.SemaphoreType.DMA((count - 1, 2)),
+        ],
+        compiler_params=pltpu.CompilerParams(
+            vmem_limit_bytes=60 * 1024 * 1024, collective_id=0, has_side_effects=True
+        ),
+    )(tokens, latents, read_weights, later_weights, head_scale)
+
+
 def solution(mesh):
     placed = (
         P(("vid", "seq"), None),
@@ -263,8 +580,10 @@
         P(None, "seq", None),
         P(),
     )
+    count = mesh.shape["seq"]
+    form = cube if count == 2**3 else gathered
     return jax.shard_map(
-        functools.partial(gathered, mesh.shape["seq"]),
+        functools.partial(form, count),
         mesh=mesh,
         in_specs=placed,
         out_specs=(P(("vid", "seq"), None), P(("vid", "seq"), None)),

time: 222 us -> 138 us (0.62)
  waiting for transfers between devices: 73.7 us -> 0 us
  Pallas kernels: 73.2 us -> 134 us
  blocking collectives: 35.5 us -> 0 us
  local copies, waits for them, and re-layouts: 18.6 us -> 3.37 us
  between operations: 13.8 us -> 0.65 us
  starting transfers between devices: 6.82 us -> 0 us
    all_gather x3 -> x0, waiting for transfers between devices: 72.3 us -> none  [the longest x1 29.7 us: gathered(): read_full = lax.all_gather(read_weights, 'seq', axis=1, tiled=True)]
    pallas_call x4 -> x1, Pallas kernels: 73.2 us -> 134 us  [cube(): pl.pallas_call(functools.partial(whole_body, count), out_shape=[jax.Shape...]
    all_gather x2 -> x0, blocking collectives: 24.4 us -> none  [the longest x1 12.8 us: gathered(): lat_all = lax.all_gather(latents, 'seq', axis=0, tiled=True)]
    slice x3 -> x0, local copies, waits for them, and re-layouts: 12.9 us -> none  [the longest x1 4.87 us: gathered(): later_full[4:]]
    all_to_all x1 -> x0, blocking collectives: 11.1 us -> none  [gathered(): lax.all_to_all(stats.reshape(count, own, LANES), 'seq', split_axis=0, con...]
    all_to_all x1 -> x0, starting transfers between devices: 6.74 us -> none  [gathered(): lax.all_to_all(parts.reshape(count, own, width), 'seq', split_axis=0, con...]
    squeeze x2 -> x0, local copies, waits for them, and re-layouts: 4.77 us -> none  [the longest x1 2.41 us: gathered(): read_full[3]]
    unnamed x4, local copies, waits for them, and re-layouts: 0.91 us -> 3.37 us
  transfers between devices with their start and end apart: 4 -> 0, of which waited for: 3 -> 0; matrix products, arithmetic and copies ran while one was open for 8% -> 0% of each run, Pallas kernels for 11% -> 0%
where the time goes in v2:
time: 138 us
  Pallas kernels  134 us (97%)
  local copies, waits for them, and re-layouts  3.37 us (2%)
    pallas_call x1, Pallas kernels, cube(): pl.pallas_call(functools.partial(whole_body, count), out_shape=[jax.Shape...  134 us
    unnamed x4, local copies, waits for them, and re-layouts  3.37 us

profile of v2, /device:TPU:1, one launch (start us, length us, event | category | flops | bytes accessed | tf_op | source)
XLA Modules:
  0.0 138.0 jit_solution(6691752232504628994)
XLA Ops:
  0.6 134.0 %shard_map.68 = (bf16[1024,768]{1,0:T(8,128)(2,1)}, f32[64,768]{1,0:T(8,128)}) custom-call(bf16[1024,768]{1,0:T(8,128)(2,1)} %tok_ref.1, bf16[64,768]{1,0:T(8,128)(2,1)} %lat_ref.1, bf16[4,96,768]{2,1,0:T(8,128)(2,1)} %rw_ref.1, bf16[8,96,768]{2,1,0:T(8,128)(2,1)} %lw_ref.1, f32[3,12]{1,0:T(4,128)} %scale_ref.1), custom_call_target="tpu_custom_call" | custom-call | tf_op jit(solution)/shard_map/pallas_call | solution.py:536
  134.6 0.0 copy-start
  134.6 2.7 %copy.9 = bf16[1024,768]{1,0:T(8,128)(2,1)} copy(bf16[1024,768]{1,0:T(8,128)(2,1)} %get-tuple-element.4) | data formatting | bytes 3145728
  137.3 0.0 copy-done
  137.3 0.7 copy.10
Async XLA Ops:
  134.6 2.7 %copy-start = (f32[64,768]{1,0:T(8,128)S(1)}, f32[64,768]{1,0:T(8,128)}, u32[]{:S(2)}) copy-start(f32[64,768]{1,0:T(8,128)} %get-tuple-element.5) | copy-start | bytes 589828

commit v3 on v2

--- a/solution.py
+++ b/solution.py
@@ -269,11 +269,11 @@
 
 
 class Gather:
-    def __init__(self, source, place, rows, sems, item, spots):
+    def __init__(self, source, place, rows, sems, item, spots, pair=None):
         send, recv = sems
         me, core, along_x, along_y, diagonal = spots
-        half = rows // 2
         self.done = set()
+        self.paired = pair is not None
 
         def copy(kind, src, dst, target):
             return pltpu.make_async_remote_copy(
@@ -281,67 +281,93 @@
                 dst_ref=dst,
                 send_sem=send.at[item, kind],
                 recv_sem=recv.at[item, kind],
-                device_id={"seq": target},
+                device_id=target,
                 device_id_type=pl.DeviceIdType.MESH,
             )
 
+        unit = rows // 3 if self.paired else rows // 2
+        base = pair[0] * unit if self.paired else 0
+
         def block(owner, start=0, size=rows):
-            return place(pl.ds(pl.multiple_of(owner * rows + start, half), size))
-
+            return place(pl.ds(pl.multiple_of(owner * rows + start, unit), size))
+
+        def both(owner, start, size):
+            return block(owner, start, size), block(owner, start, size)
+
+        x_dev, y_dev, core_dev = {"seq": along_x}, {"seq": along_y}, {"seq": core}
         mine = source if source is not None else block(me)
+        share = block(me, base, 2 * unit)
+        if source is None:
+            part = share
+        else:
+            part = source.at[pl.ds(pl.multiple_of(base, unit), 2 * unit)]
         self.first = [
-            copy(0, mine, block(me), along_x),
-            copy(1, mine, block(me), along_y),
-            copy(2, mine, block(me), core),
+            copy(0, part, share, x_dev),
+            copy(1, part, share, y_dev),
+            copy(2, mine, block(me), core_dev),
         ]
         self.relay = [
-            copy(3, block(along_x, 0, half), block(along_x, 0, half), along_y),
-            copy(4, block(along_y, half, half), block(along_y, half, half), along_x),
-            copy(5, block(along_x), block(along_x), core),
-            copy(6, block(along_y), block(along_y), core),
+            copy(3, *both(along_x, base, unit), y_dev),
+            copy(4, *both(along_y, base + unit, unit), x_dev),
         ]
-        self.last = [copy(7, block(diagonal), block(diagonal), core)]
+        self.forward = [
+            copy(5 + i, *both(owner, 0, rows), core_dev)
+            for i, owner in enumerate((along_x, along_y, diagonal))
+        ]
+        self.swap = []
+        if self.paired:
+            self.swap = [
+                copy(8 + i, *both(owner, pair[0] * 2 * unit, unit), {"vid": pair[1]})
+                for i, owner in enumerate((along_x, along_y, diagonal))
+            ]
         self.local = None
         if source is not None:
-            self.local = pltpu.make_async_copy(source, block(me), send.at[item, 8])
+            self.local = pltpu.make_async_copy(source, block(me), send.at[item, 11])
+
+    def once(self, stage):
+        fresh = stage not in self.done
+        self.done.add(stage)
+        return fresh
 
     def start(self):
-        if "start" not in self.done:
-            self.done.add("start")
+        if self.once("start"):
             for copy in self.first:
                 copy.start()
             if self.local is not None:
                 self.local.start()
 
     def spread(self):
-        if "spread" not in self.done:
-            self.done.add("spread")
-            self.first[0].wait_recv()
-            self.relay[0].start()
-            self.relay[2].start()
-            self.first[1].wait_recv()
-            self.relay[1].start()
-            self.relay[3].start()
+        if self.once("spread"):
+            onward = self.swap if self.paired else self.forward
+            for i in range(2):
+                self.first[i].wait_recv()
+                self.relay[i].start()
+                onward[i].start()
 
     def close(self):
-        if "close" not in self.done:
-            self.done.add("close")
+        if self.once("close"):
             self.relay[0].wait_recv()
             self.relay[1].wait_recv()
-            self.last[0].start()
+            (self.swap if self.paired else self.forward)[2].start()
+
+    def settle(self):
+        if self.paired and self.once("settle"):
+            for i in range(3):
+                self.swap[i].wait_recv()
+                self.forward[i].start()
 
     def need(self):
         self.spread()
         self.close()
+        self.settle()
         self.first[2].wait_recv()
-        self.relay[2].wait_recv()
-        self.relay[3].wait_recv()
-        self.last[0].wait_recv()
+        for copy in self.forward:
+            copy.wait_recv()
         if self.local is not None:
             self.local.wait()
 
     def drain(self):
-        for copy in self.first + self.relay + self.last:
+        for copy in self.first + self.relay + self.forward + self.swap:
             copy.wait_send()
 
 
@@ -369,11 +395,16 @@
             barrier, inc=1, device_id={"seq": (me + step) % count},
             device_id_type=pl.DeviceIdType.MESH,
         )
-    pl.semaphore_wait(barrier, count - 1)
+    plane = lax.axis_index("vid")
+    pair = (plane % 2, plane + 1 - 2 * (plane % 2))
+    pl.semaphore_signal(
+        barrier, inc=1, device_id={"vid": pair[1]}, device_id_type=pl.DeviceIdType.MESH
+    )
+    pl.semaphore_wait(barrier, count)
 
     def matrix(item, index):
         source = rw_ref.at[index] if index < n_read else lw_ref.at[index - n_read]
-        return Gather(source, lambda rows: w_ref.at[index, rows], shard, sems, item, spots)
+        return Gather(source, lambda rows: w_ref.at[index, rows], shard, sems, item, spots, pair)
 
     def array(item, source, ref):
         return Gather(source, lambda rows: ref.at[rows], own, sems, item, spots)
@@ -397,7 +428,10 @@
     stats_ref[...] = jnp.zeros(stats_ref.shape, F32)
     r1.spread()
     r0.start()
+    r1.close()
     r2.spread()
+    l4.start()
+    r2.close()
     r1.need()
 
     def key_rows(here):
@@ -405,7 +439,7 @@
 
     by_rows(slab, 256, key_rows)
     lat.spread()
-    l4.start()
+    r3.start()
     r2.need()
 
     def value_rows(here):
@@ -414,11 +448,12 @@
     by_rows(slab, 256, value_rows)
     lat.close()
     r0.spread()
-    r3.start()
+    l0.start()
+    r0.close()
+    l4.spread()
     lat.need()
     r0.need()
-    l4.spread()
-    l0.start()
+    l4.close()
 
     def query_rows(here):
         normed = rms(lat_all[here, :].astype(F32)).astype(BF16)
@@ -433,38 +468,60 @@
 
         return body
 
+    sums = []
+
+    def exchange(src, dst, cols, kind):
+        copies = []
+        for step in range(1, count):
+            target = (me + step) % count
+            rows = pl.ds(pl.multiple_of(target * own, own), own)
+            copies.append(
+                pltpu.make_async_remote_copy(
+                    src_ref=src.at[rows, cols],
+                    dst_ref=dst.at[step - 1, :, cols],
+                    send_sem=slab_send.at[step - 1, kind],
+                    recv_sem=slab_recv.at[step - 1, kind],
+                    device_id={"seq": target},
+                    device_id_type=pl.DeviceIdType.MESH,
+                )
+            )
+        sums.extend(copies)
+
+        def body():
+            for copy in copies:
+                copy.start()
+
+        return body
+
+    third = width // 3
+    groups = [
+        exchange(parts_ref, got_ref, slice(i * third, i * third + third), i) for i in range(3)
+    ]
     attention(
-        q_ref, k_ref, v_ref, scale_ref, 0, parts_ref, stats_ref, 256,
+        q_ref, k_ref, v_ref, scale_ref, 0, parts_ref, stats_ref, lat_all.shape[0] // 2,
         {
-            0: run(l4.close, r3.spread, l1.start),
-            3: run(r3.close, l0.spread, l2.start),
-            6: run(l0.close, l1.spread),
-            9: run(l1.close, l2.spread),
+            0: run(l4.settle, r3.spread, l1.start),
+            2: run(r3.close, l0.spread, l2.start),
+            4: run(groups[0], r3.settle, l0.close, l1.spread, l3.start),
+            6: run(l0.settle, l1.close, l2.spread, l5.start),
+            8: run(groups[1], l1.settle, l2.close, l3.spread, l6.start),
+            10: run(l2.settle, l3.close, l5.spread, l7.start),
         },
     )
-    sums = []
-    for step in range(1, count):
-        target = (me + step) % count
-        rows = pl.ds(pl.multiple_of(target * own, own), own)
-        for kind, (src, dst) in enumerate(((parts_ref, got_ref), (stats_ref, got_stats))):
-            copy = pltpu.make_async_remote_copy(
-                src_ref=src.at[rows],
-                dst_ref=dst.at[step - 1],
-                send_sem=slab_send.at[step - 1, kind],
-                recv_sem=slab_recv.at[step - 1, kind],
-                device_id={"seq": target},
-                device_id_type=pl.DeviceIdType.MESH,
-            )
-            copy.start()
-            sums.append(copy)
-    l2.close()
-    l3.start()
+    groups[2]()
+    exchange(stats_ref, got_stats, slice(0, LANES), 3)()
+    l3.settle()
+    l5.close()
+    l6.spread()
     l4.need()
 
     def write_query_rows(here):
         wq_ref[here, :] = head_norm(dot(norm_ref[here, :], w_ref[n_read + 4]), group)
 
     by_rows(slab, 256, write_query_rows)
+    l5.settle()
+    l6.close()
+    l7.spread()
     for item in (r3, l0, l1, l2):
         item.need()
     for copy in sums:
@@ -477,10 +534,8 @@
         one_ref, self_q, kv_ref.at[mine],
     )
     kv.start()
-    l3.spread()
-    l5.start()
-    l6.start()
-    l3.close()
+    l6.settle()
+    l7.close()
     kv.need()
     attention(
         self_q, kv_ref.at[:, :width], kv_ref.at[:, width:], scale_ref, 1, mix_small, None, own
@@ -490,12 +545,7 @@
     lat_out_ref[...] = latents_out
     in_ref[mine, :] = rms(latents_out).astype(BF16)
     into.start()
-    l5.spread()
-    l6.spread()
-    l7.start()
-    into.spread()
-    l5.close()
-    l6.close()
+    l7.settle()
     into.need()
     l5.need()
 
@@ -509,8 +559,7 @@
     l6.need()
     by_rows(lat_all.shape[0], 256, write_value_rows)
     attention(
-        wq_ref, wk_ref, wv_ref, scale_ref, 2, mix_ref, None, 256,
-        {2: l7.spread, 6: l7.close},
+        wq_ref, wk_ref, wv_ref, scale_ref, 2, mix_ref, None, 256
     )
     l7.need()
 
@@ -561,10 +610,10 @@
             vmem(rows, width),
             vmem(rows, width),
             vmem(slab, width),
-            pltpu.SemaphoreType.DMA((matrices + 3, 9)),
-            pltpu.SemaphoreType.DMA((matrices + 3, 8)),
-            pltpu.SemaphoreType.DMA((count - 1, 2)),
-            pltpu.SemaphoreType.DMA((count - 1, 2)),
+            pltpu.SemaphoreType.DMA((matrices + 3, 12)),
+            pltpu.SemaphoreType.DMA((matrices + 3, 11)),
+            pltpu.SemaphoreType.DMA((count - 1, 4)),
+            pltpu.SemaphoreType.DMA((count - 1, 4)),
         ],
         compiler_params=pltpu.CompilerParams(
             vmem_limit_bytes=60 * 1024 * 1024, collective_id=0, has_side_effects=True
@@ -581,7 +630,7 @@
         P(),
     )
     count = mesh.shape["seq"]
-    form = cube if count == 2**3 else gathered
+    form = cube if count == 2**3 and mesh.shape["vid"] % 2 == 0 else gathered
     return jax.shard_map(
         functools.partial(form, count),
         mesh=mesh,

time: 138 us -> 134 us (0.971)
  Pallas kernels: 134 us -> 130 us
    pallas_call x1, Pallas kernels: 134 us -> 130 us  [cube(): pl.pallas_call(functools.partial(whole_body, count), out_shape=[jax.Shape...]
where the time goes in v3:
time: 134 us
  Pallas kernels  130 us (97%)
  local copies, waits for them, and re-layouts  3.37 us (3%)
    pallas_call x1, Pallas kernels, cube(): pl.pallas_call(functools.partial(whole_body, count), out_shape=[jax.Shape...  130 us
    unnamed x4, local copies, waits for them, and re-layouts  3.37 us

profile of v3, /device:TPU:1, one launch (start us, length us, event | category | flops | bytes accessed | tf_op | source)
XLA Modules:
  0.0 134.3 jit_solution(3379803439517888360)
XLA Ops:
  0.6 130.3 %shard_map.68 = (bf16[1024,768]{1,0:T(8,128)(2,1)}, f32[64,768]{1,0:T(8,128)}) custom-call(bf16[1024,768]{1,0:T(8,128)(2,1)} %tok_ref.1, bf16[64,768]{1,0:T(8,128)(2,1)} %lat_ref.1, bf16[4,96,768]{2,1,0:T(8,128)(2,1)} %rw_ref.1, bf16[8,96,768]{2,1,0:T(8,128)(2,1)} %lw_ref.1, f32[3,12]{1,0:T(4,128)} %scale_ref.1), custom_call_target="tpu_custom_call" | custom-call | tf_op jit(solution)/shard_map/pallas_call | solution.py:585
  130.9 0.0 copy-start
  130.9 2.7 %copy.9 = bf16[1024,768]{1,0:T(8,128)(2,1)} copy(bf16[1024,768]{1,0:T(8,128)(2,1)} %get-tuple-element.4) | data formatting | bytes 3145728
  133.6 0.0 copy-done
  133.6 0.7 copy.10
Async XLA Ops:
  130.9 2.7 %copy-start = (f32[64,768]{1,0:T(8,128)S(1)}, f32[64,768]{1,0:T(8,128)}, u32[]{:S(2)}) copy-start(f32[64,768]{1,0:T(8,128)} %get-tuple-element.5) | copy-start | bytes 589828

commit v4 on v3

--- a/solution.py
+++ b/solution.py
@@ -98,15 +98,14 @@
             top = jnp.max(scores, axis=1, keepdims=True)
             exp_scores = jnp.exp2((scores - top) * (factor * LOG2E))
             total = jnp.sum(exp_scores, axis=1, keepdims=True)
-            if stats_ref is None:
-                weights = (exp_scores * (1.0 / total)).astype(BF16)
-            else:
-                weights = exp_scores.astype(BF16)
+            weights = exp_scores.astype(BF16)
+            if stats_ref is not None:
                 lane = lax.broadcasted_iota(jnp.int32, (chunk, LANES), 1)
                 old = stats_ref[here, :]
                 old = jnp.where(lane == head, top * factor, old)
                 stats_ref[here, :] = jnp.where(lane == head + LANES // 2, total, old)
-            results.append(dot(weights, v))
+            mixed = dot(weights, v)
+            results.append(mixed / total if stats_ref is None else mixed)
         out_ref[here, cols] = merge_halves(results, head_dim).astype(BF16)
         return carry
 
@@ -419,6 +418,7 @@
     r1.start()
     r2.start()
     lat.start()
+    r0.start()
 
     def norm_rows(here):
         norm_ref[here, :] = rms(tok_ref[here, :].astype(F32)).astype(BF16)
@@ -427,10 +427,10 @@
     by_rows(slab, 256, norm_rows)
     stats_ref[...] = jnp.zeros(stats_ref.shape, F32)
     r1.spread()
-    r0.start()
+    l4.start()
     r1.close()
     r2.spread()
-    l4.start()
+    r3.start()
     r2.close()
     r1.need()
 
@@ -439,7 +439,7 @@
 
     by_rows(slab, 256, key_rows)
     lat.spread()
-    r3.start()
+    l0.start()
     r2.need()
 
     def value_rows(here):
@@ -448,7 +448,7 @@
     by_rows(slab, 256, value_rows)
     lat.close()
     r0.spread()
-    l0.start()
+    l1.start()
     r0.close()
     l4.spread()
     lat.need()
@@ -500,12 +500,12 @@
     attention(
         q_ref, k_ref, v_ref, scale_ref, 0, parts_ref, stats_ref, lat_all.shape[0] // 2,
         {
-            0: run(l4.settle, r3.spread, l1.start),
-            2: run(r3.close, l0.spread, l2.start),
-            4: run(groups[0], r3.settle, l0.close, l1.spread, l3.start),
-            6: run(l0.settle, l1.close, l2.spread, l5.start),
-            8: run(groups[1], l1.settle, l2.close, l3.spread, l6.start),
-            10: run(l2.settle, l3.close, l5.spread, l7.start),
+            0: run(l4.settle, r3.spread, l2.start),
+            2: run(r3.close, l0.spread, l3.start),
+            4: run(groups[0], r3.settle, l0.close, l1.spread, l5.start),
+            6: run(l0.settle, l1.close, l2.spread, l6.start),
+            8: run(groups[1], l1.settle, l2.close, l3.spread, l7.start),
+            10: run(l2.settle, l3.close, l5.spread),
         },
     )
     groups[2]()

time: 134 us -> 129 us (0.963)
  Pallas kernels: 130 us -> 124 us
    pallas_call x1, Pallas kernels: 130 us -> 124 us  [cube(): pl.pallas_call(functools.partial(whole_body, count), out_shape=[jax.Shape...]
where the time goes in v4:
time: 129 us; the launch traced here: 128 us
  Pallas kernels  124 us (96%)
  local copies, waits for them, and re-layouts  3.37 us (3%)
    pallas_call x1, Pallas kernels, cube(): pl.pallas_call(functools.partial(whole_body, count), out_shape=[jax.Shape...  124 us
    unnamed x4, local copies, waits for them, and re-layouts  3.37 us

profile of v4, /device:TPU:1, one launch (start us, length us, event | category | flops | bytes accessed | tf_op | source)
XLA Modules:
  0.0 128.4 jit_solution(3257452206749638278)
XLA Ops:
  0.6 124.4 %shard_map.68 = (bf16[1024,768]{1,0:T(8,128)(2,1)}, f32[64,768]{1,0:T(8,128)}) custom-call(bf16[1024,768]{1,0:T(8,128)(2,1)} %tok_ref.1, bf16[64,768]{1,0:T(8,128)(2,1)} %lat_ref.1, bf16[4,96,768]{2,1,0:T(8,128)(2,1)} %rw_ref.1, bf16[8,96,768]{2,1,0:T(8,128)(2,1)} %lw_ref.1, f32[3,12]{1,0:T(4,128)} %scale_ref.1), custom_call_target="tpu_custom_call" | custom-call | tf_op jit(solution)/shard_map/pallas_call | solution.py:585
  125.0 0.0 copy-start
  125.1 2.7 %copy.9 = bf16[1024,768]{1,0:T(8,128)(2,1)} copy(bf16[1024,768]{1,0:T(8,128)(2,1)} %get-tuple-element.4) | data formatting | bytes 3145728
  127.7 0.0 copy-done
  127.8 0.7 copy.10
Async XLA Ops:
  125.0 2.7 %copy-start = (f32[64,768]{1,0:T(8,128)S(1)}, f32[64,768]{1,0:T(8,128)}, u32[]{:S(2)}) copy-start(f32[64,768]{1,0:T(8,128)} %get-tuple-element.5) | copy-start | bytes 589828
